TPU v7x, 256 devices: a whole 4x4x8 slice. The times are simulated.
256 devices in a mesh: leaf: 16 (over y, x), col: 16 (over z, core).
Axes of the slice: x: 4, y: 4, z: 8, core: 2. Of those that a mesh axis runs over, the one named last changes fastest.
Arguments:
- right_sides: bfloat16 [16, 2, 1792, 128], P('leaf', None, 'col'), may hold values from -6 to 6
- leaf_inverse: bfloat16 [16, 1792, 1792], P('leaf', 'col'), as said below
- upper_inverse: bfloat16 [16, 1792, 1792], P('leaf', 'col'), as said below
- leaf_update: bfloat16 [16, 4, 1792, 512], P('leaf', None, 'col'), may hold values from -0.0625 to 0.0625
- upper_update: bfloat16 [16, 4, 1792, 512], P('leaf', None, 'col'), may hold values from -0.0625 to 0.0625
- live_rows: int32 [16, 2], P('leaf'), may hold values from 896 to 1792, as said below
- tile_map: int32 [16, 2, 4, 512], P('leaf'), may hold values from 0 to 1791, as said below
Outputs:
- solution: bfloat16 [16, 2, 1792, 128], P('leaf', None, 'col')
Inputs may be any that keep to these rules, and one draw needn't show every extreme that they name: `leaf_inverse`: zero above the diagonal, nonzero on it. `upper_inverse`: zero above the diagonal, nonzero on it. `live_rows`: one supernode has all 1792 rows live and one has 896. `tile_map`: the rows of one tile are distinct and increasing.
All inputs are finite; a program needn't handle non-finite values.
Results may differ from a plain program's by a relative error of at most 0.0075.
Values may be sent and summed in bfloat16 or wider, within the bound.
No kernel may reach another device: no remote copies, remote signals or barrier semaphores. Data moves between devices by JAX's collectives and lax.ppermute only.
A program may use at most 64 MiB of HBM per device.

v0:
```python
import jax
import jax.numpy as jnp
from jax import lax
from jax.sharding import PartitionSpec as P

BF = jnp.bfloat16
F32 = jnp.float32


def dot(a, b, ca, cb):
    return lax.dot_general(a, b, (((ca,), (cb,)), ((), ())), preferred_element_type=F32)


def split_dot(a, b, ca, cb):
    hi = a.astype(BF)
    lo = (a - hi.astype(F32)).astype(BF)
    n = a.shape[0]
    both = dot(jnp.concatenate([hi, lo], axis=0), b, ca, cb)
    return both[:n] + both[n:]


def shards(
    right_sides, leaf_inverse, upper_inverse, leaf_update, upper_update, live_rows, tile_map
):
    leaf_count = lax.axis_size("leaf")
    col_count = lax.axis_size("col")
    depth = leaf_count.bit_length() - 1
    rows_dev = leaf_inverse.shape[1]
    rows = leaf_inverse.shape[2]
    width = right_sides.shape[3]
    part = width // col_count
    tile_len = tile_map.shape[3]
    leaf_id = lax.axis_index("leaf")
    col_id = lax.axis_index("col")
    all_rows = lax.broadcasted_iota(jnp.int32, (1, rows), 1)
    mask_up = (all_rows < live_rows[0, 1]).astype(F32)
    rows_full = lax.broadcasted_iota(jnp.int32, (rows, 1), 0)
    own_rows = col_id * rows_dev + lax.broadcasted_iota(jnp.int32, (rows_dev, 1), 0)
    mask_leaf = (own_rows < live_rows[0, 0]).astype(F32)
    node_level = jnp.zeros((), jnp.int32)
    for height in range(1, depth + 1):
        node_level = node_level + ((leaf_id % 2 ** (height - 1) == 0) & (leaf_id > 0)).astype(
            jnp.int32
        )
    inv_up = lax.all_gather(upper_inverse[0], "col", axis=0, tiled=True)
    upd_up = lax.all_gather(upper_update[0, : depth - 1], "col", axis=1, tiled=True)
    picks = (
        tile_map[0][:, :, :, None] == lax.broadcasted_iota(jnp.int32, (1, 1, 1, rows), 3)
    ).astype(BF)
    pick_leaf, pick_up = (picks[0], picks[1])
    both = lax.all_gather(right_sides[0], "col", axis=1, tiled=True)
    r_leaf = jnp.where(rows_full < live_rows[0, 0], both[0], jnp.zeros_like(both[0]))
    base_up = lax.dynamic_slice_in_dim(both[1].T, col_id * part, part, 0).astype(F32)
    y_leaf = (dot(leaf_inverse[0], r_leaf, 1, 0) * mask_leaf).astype(BF)
    terms = jnp.concatenate(
        [dot(y_leaf, leaf_update[0, s], 0, 0) for s in range(depth)], axis=1
    ).astype(BF)
    swapped = lax.all_to_all(
        terms.reshape(col_count, part, depth * tile_len), "col", 0, 0, tiled=False
    )
    z_leaf = jnp.sum(swapped.astype(F32), axis=0)
    acc = jnp.stack(
        [
            split_dot(z_leaf[:, s * tile_len : (s + 1) * tile_len], pick_leaf[s], 1, 0)
            for s in range(depth)
        ]
    )
    nodes = range(1, leaf_count)

    def level_of(node):
        return (node & -node).bit_length()

    y_up = jnp.zeros((part, rows), BF)
    for height in range(1, depth + 1):
        if height == 1:
            got = lax.ppermute(acc, "leaf", [(i, i + 1) for i in range(0, leaf_count, 2)])
            acc = jnp.where(leaf_id % 2 == 1, acc + got, 0.0)
        else:
            step = 2 ** (height - 2)
            ups = [i for i in nodes if level_of(i) == height]
            acc = lax.ppermute(acc, "leaf", [(i - step, i) for i in ups]) + lax.ppermute(
                acc, "leaf", [(i + step, i) for i in ups]
            )
        r = ((base_up - acc[0]) * mask_up).astype(BF)
        y = (dot(r, inv_up, 1, 1) * mask_up).astype(BF)
        y_up = jnp.where(node_level == height, y, y_up)
        acc = acc[1:]
        if height < depth:
            acc = acc + jnp.stack(
                [
                    split_dot(dot(y, upd_up[s], 1, 0), pick_up[s], 1, 0)
                    for s in range(depth - height)
                ]
            )
    x_up = jnp.zeros((part, rows), BF)
    above = None
    for height in range(depth, 0, -1):
        if height == depth:
            pulled = jnp.zeros((part, rows), F32)
        else:
            pulled = sum(
                (
                    dot(dot(above[s], pick_up[s], 1, 1).astype(BF), upd_up[s], 1, 1)
                    for s in range(depth - height)
                )
            )
        v = ((y_up.astype(F32) - pulled) * mask_up).astype(BF)
        x = (dot(v, inv_up, 1, 0) * mask_up).astype(BF)
        x_up = jnp.where(node_level == height, x, x_up)
        above = x[None] if above is None else jnp.concatenate([x[None], above])
        if height == 1:
            got = lax.ppermute(above, "leaf", [(i + 1, i) for i in range(0, leaf_count, 2)])
            above = jnp.where(leaf_id % 2 == 1, above, got)
        else:
            step = 2 ** (height - 2)
            ups = [i for i in nodes if level_of(i) == height]
            above = lax.ppermute(above, "leaf", [(i, i - step) for i in ups]) + lax.ppermute(
                above, "leaf", [(i, i + step) for i in ups]
            )
    tiles = jnp.concatenate(
        [dot(above[s], pick_leaf[s], 1, 1).astype(BF) for s in range(depth)], axis=1
    )
    tiles = lax.all_gather(tiles, "col", axis=0, tiled=True)
    pulled = sum(
        (
            dot(leaf_update[0, s], tiles[:, s * tile_len : (s + 1) * tile_len], 1, 1)
            for s in range(depth)
        )
    )
    v = ((y_leaf.astype(F32) - pulled) * mask_leaf).astype(BF)
    terms = dot(leaf_inverse[0], v, 0, 0).astype(BF).reshape(col_count, rows_dev, width)
    swapped = lax.all_to_all(terms, "col", 0, 0, tiled=False)
    x_leaf = (jnp.sum(swapped.astype(F32), axis=0) * mask_leaf).astype(BF)
    x_up = jnp.where(leaf_id > 0, x_up, jnp.zeros_like(x_up))
    up_rows = lax.all_to_all(
        x_up.reshape(part, col_count, rows_dev).transpose(1, 0, 2), "col", 0, 0, tiled=False
    )
    up_rows = up_rows.reshape(width, rows_dev).T
    return jnp.stack([x_leaf, up_rows])[None]


def solution(mesh):
    placed = (
        P("leaf", None, "col", None),
        P("leaf", "col", None),
        P("leaf", "col", None),
        P("leaf", None, "col", None),
        P("leaf", None, "col", None),
        P("leaf", None),
        P("leaf", None, None, None),
    )
    return jax.shard_map(
        shards, mesh=mesh, in_specs=placed, out_specs=P("leaf", None, "col", None), check_vma=False
    )
```

profile of v0, /device:TPU:23, one launch (start us, length us, event | category | flops | bytes accessed | tf_op | source)
XLA Modules:
  0.0 273.4 jit_solution(10136190612062378976)
XLA Ops:
  7.3 1.7 slice.255
  10.0 1.3 fusion.229
  12.5 25.3 %all-gather = bf16[1,2,1792,128]{3,1,0,2:T(2,128)(2,1)S(1)} all-gather(bf16[1,2,112,128]{3,1,0,2:T(2,128)(2,1)S(1)} %copy.25), channel_id=2, replica_groups=mesh['leaf'=16,'col'=16] {'col'}, dimensions={2}, use_global_device_ids=true | all-gather | bytes 974848 | tf_op jit(solution)/shard_map/all_gather | solution.py:51
  37.9 1.3 fusion.228
  42.0 4.2 %all-to-all-start = ((bf16[16,8,2048]{2,1,0:T(8,128)(2,1)}), bf16[16,8,2048]{2,1,0:T(8,128)(2,1)S(1)}, u32[]{:S(2)}, u32[]{:S(2)}) async-start(bf16[16,8,2048]{2,1,0:T(8,128)(2,1)} %pad_maximum_fusion), calls=%async_computation | async-start | bytes 1048576 | tf_op jit(solution)/shard_map/all_to_all | solution.py:58
  46.2 6.7 %iota_compare_fusion = pred[2,4,512,1792]{3,2,1,0:T(32,128)(4,1)} fusion(s32[2,4,512]{2,1,0:T(4,128)S(1)} %bitcast.352), kind=kLoop, calls=%fused_computation | loop fusion | flops 7340032 | bytes 7356416 | tf_op jit(solution)/shard_map/eq | solution.py:48
  52.9 1.6 slice_bitcast_fusion.2
  54.5 14.0 %all-to-all-done = bf16[16,8,2048]{2,1,0:T(8,128)(2,1)S(1)} async-done(((bf16[16,8,2048]{2,1,0:T(8,128)(2,1)}), bf16[16,8,2048]{2,1,0:T(8,128)(2,1)S(1)}, u32[]{:S(2)}, u32[]{:S(2)}) %all-to-all-start) | async-done | bytes 524320 | tf_op jit(solution)/shard_map/all_to_all | solution.py:58
  68.6 1.8 fusion.17
  70.5 1.8 fusion.19
  72.3 1.8 fusion.21
  74.1 1.8 fusion.23
  76.7 1.3 collective-permute-start
  78.0 1.2 constant_dynamic-slice_fusion
  80.5 5.4 %collective-permute-done = f32[4,8,1792]{2,1,0:T(8,128)} collective-permute-done((f32[4,8,1792]{2,1,0:T(8,128)}, f32[4,8,1792]{2,1,0:T(8,128)}, u32[]{:S(2)}, u32[]{:S(2)}) %collective-permute-start) | collective-permute-done | bytes 229408 | tf_op jit(solution)/shard_map/ppermute | solution.py:76
  87.6 5.3 %fusion.77 = bf16[8,1792]{1,0:T(8,128)(2,1)} fusion(bf16[1,1792,1792]{2,1,0:T(8,128)(2,1)} %all-gather.6.cloned.1.call-done, f32[4,8,1792]{2,1,0:T(8,128)S(1)} %add_select_fusion, bf16[1,1,1792,8]{2,3,1,0:T(8,128)(2,1)S(1)} %copy.34, f32[1792]{0:T(1024)S(1)} %fusion.216), kind=kOutput, calls=%fused_computation.60 | convolution fusion | flops 51466240 | bytes 6553600 | tf_op jit(solution)/shard_map/dot_general | solution.py:11
  93.0 23.7 %all-gather.8.cloned.1.call-done = bf16[1,3,1792,512]{3,2,1,0:T(8,128)(2,1)} async-done(((bf16[1,3,112,512]{3,2,1,0:T(8,128)(2,1)}), bf16[1,3,1792,512]{3,2,1,0:T(8,128)(2,1)}) %all-gather.8.cloned.1.call-update) | async-done | bytes 5505040 | tf_op jit(solution)/shard_map/all_gather | solution.py:46
  116.6 2.0 subtract_convert_fusion.5
  119.2 1.9 subtract_convert_fusion.4
  121.1 2.0 fusion.104
  123.0 1.1 subtract_convert_fusion.3
  124.1 1.8 fusion.25
  126.7 3.1 %collective-permute-start.2 = (f32[3,8,1792]{2,1,0:T(8,128)S(1)}, f32[3,8,1792]{2,1,0:T(8,128)S(1)}, u32[]{:S(2)}, u32[]{:S(2)}) collective-permute-start(f32[3,8,1792]{2,1,0:T(8,128)S(1)} %slice_add_fusion), channel_id=1, source_target_pairs={{48,32},{112,96},{176,160},{240,224},{49,33},{113,97},{177,161},{2... | collective-permute-start | bytes 516104 | tf_op jit(solution)/shard_map/ppermute | solution.py:81
  129.8 3.4 %collective-permute-done.2 = f32[3,8,1792]{2,1,0:T(8,128)S(1)} collective-permute-done((f32[3,8,1792]{2,1,0:T(8,128)S(1)}, f32[3,8,1792]{2,1,0:T(8,128)S(1)}, u32[]{:S(2)}, u32[]{:S(2)}) %collective-permute-start.2) | collective-permute-done | bytes 172064 | tf_op jit(solution)/shard_map/ppermute | solution.py:81
  133.3 1.8 fusion.74
  136.3 1.8 fusion.103
  139.8 1.8 fusion.71
  143.9 4.6 %fusion.86 = f32[8,1792]{1,0:T(8,128)S(1)} fusion(bf16[1,1792,1792]{2,1,0:T(8,128)(2,1)} %all-gather.6.cloned.1.call-done, f32[1,8,1792]{2,1,0:T(8,128)S(1)} %collective-permute-done.5, f32[1,8,1792]{2,1,0:T(8,128)S(1)} %collective-permute-done.6, bf16[1,1,1792,8]{2,3,1,0:T(8,128)(2,1)} %copy-done.6, bf16[8,1792]{1,0:T(8,128)(2,1)} %copy-done.9, ...), kind=kOutput, calls=%fused_computation.65 | convolution fusion | flops 51552256 | bytes 6716420 | tf_op jit(solution)/shard_map/dot_general | solution.py:11
  148.5 3.8 %fusion.65 = bf16[8,1792]{1,0:T(8,128)(2,1)S(1)} fusion(bf16[1,1792,1792]{2,1,0:T(8,128)(2,1)} %all-gather.6.cloned.1.call-done, f32[8,1792]{1,0:T(8,128)S(1)} %fusion.86, f32[1792]{0:T(1024)S(1)} %fusion.216), kind=kOutput, calls=%fused_computation.56 | convolution fusion | flops 51437568 | bytes 6515712 | tf_op jit(solution)/shard_map/dot_general | solution.py:11
  154.3 4.9 %fusion.62 = bf16[8,1792]{1,0:T(8,128)(2,1)S(1)} fusion(bf16[1,1792,1792]{2,1,0:T(8,128)(2,1)} %all-gather.6.cloned.1.call-done, f32[8,1792]{1,0:T(8,128)S(1)} %fusion.86, bf16[8,512]{1,0:T(8,128)(2,1)S(1)} %convolution_convert_fusion.9, bf16[1,3,1792,512]{3,2,1,0:T(8,128)(2,1)} %all-gather.8.cloned.1.call-done, f32[1792]{0:T(1024)S(1)} %fusion.216), kind=kOutput, calls=%fused_computation.55 | convolution fusion | flops 66131968 | bytes 8368128 | tf_op jit(solution)/shard_map/dot_general | solution.py:11
  160.6 2.7 fusion.101
  163.3 3.1 %fusion.81 = bf16[8,1792]{1,0:T(8,128)(2,1)S(1)} fusion(f32[8,1792]{1,0:T(8,128)S(1)} %fusion.86, f32[8,1792]{1,0:T(8,128)S(1)} %fusion.101, bf16[1,3,1792,512]{3,2,1,0:T(8,128)(2,1)} %all-gather.8.cloned.1.call-done, pred[2,4,512,1792]{3,2,1,0:T(32,128)(4,1)} %iota_compare_fusion, bf16[2,8,1792]{2,1,0:T(8,128)(2,1)S(1)} %add.144, f32[1792]{0:T(1024)S(1)} %fusion.216), kind=kOutput, calls=%fused_computation.62 | convolution fusion | flops 29421568 | bytes 2932736 | tf_op jit(solution)/shard_map/dot_general | solution.py:11
  166.4 3.8 %fusion.59 = bf16[8,1792]{1,0:T(8,128)(2,1)S(1)} fusion(bf16[8,1792]{1,0:T(8,128)(2,1)S(1)} %fusion.81, bf16[1,1792,1792]{2,1,0:T(8,128)(2,1)} %all-gather.6.cloned.1.call-done, f32[1792]{0:T(1024)S(1)} %fusion.216), kind=kOutput, calls=%fused_computation.54 | convolution fusion | flops 51408896 | bytes 6487040 | tf_op jit(solution)/shard_map/dot_general | solution.py:11
  170.9 1.3 collective-permute-start.12
  172.2 20.2 %collective-permute-done.12 = bf16[3,8,1792]{2,1,0:T(8,128)(2,1)S(1)} collective-permute-done((bf16[3,8,1792]{2,1,0:T(8,128)(2,1)S(1)}, bf16[3,8,1792]{2,1,0:T(8,128)(2,1)S(1)}, u32[]{:S(2)}, u32[]{:S(2)}) %collective-permute-start.12) | collective-permute-done | bytes 86048 | tf_op jit(solution)/shard_map/ppermute | solution.py:117
  192.5 2.7 fusion.102
  195.1 3.1 %convolution_add_fusion.1 = f32[8,1792]{1,0:T(8,128)S(1)} fusion(f32[8,1792]{1,0:T(8,128)S(1)} %fusion.102, bf16[1,3,1792,512]{3,2,1,0:T(8,128)(2,1)} %all-gather.8.cloned.1.call-done, pred[2,4,512,1792]{3,2,1,0:T(32,128)(4,1)} %iota_compare_fusion, bf16[3,8,1792]{2,1,0:T(8,128)(2,1)S(1)} %add.146), kind=kOutput, calls=%fused_computation.39 | convolution fusion | flops 29378560 | bytes 2895872 | tf_op jit(solution)/shard_map/dot_general | solution.py:11
  198.2 3.1 %fusion.82 = bf16[8,1792]{1,0:T(8,128)(2,1)S(1)} fusion(f32[8,1792]{1,0:T(8,128)S(1)} %fusion.86, f32[8,1792]{1,0:T(8,128)S(1)} %convolution_add_fusion.1, bf16[1,3,1792,512]{3,2,1,0:T(8,128)(2,1)} %all-gather.8.cloned.1.call-done, pred[2,4,512,1792]{3,2,1,0:T(32,128)(4,1)} %iota_compare_fusion, bf16[3,8,1792]{2,1,0:T(8,128)(2,1)S(1)} %add.146, ...), kind=kOutput, calls=%fused_computation.63 | convolution fusion | flops 29421568 | bytes 2932736 | tf_op jit(solution)/shard_map/dot_general | solution.py:11
  201.4 3.8 %select_select_fusion = (bf16[8,1792]{1,0:T(8,128)(2,1)S(1)}, bf16[8,1792]{1,0:T(8,128)(2,1)S(1)}) fusion(bf16[8,1792]{1,0:T(8,128)(2,1)S(1)} %fusion.59, bf16[8,1792]{1,0:T(8,128)(2,1)S(1)} %fusion.62, bf16[8,1792]{1,0:T(8,128)(2,1)S(1)} %fusion.65, pred[]{:T(512)S(6)} %gt.2, pred[]{:T(512)S(6)} %eq.63, pred[]{:T(512)S(6)} %eq.62, pred[]{:T(512)S(6)} %eq.61, ...), kind=kOutput, calls=%fused_computation.202 | convolution fusion | flops 51480576 | bytes 6601733 | tf_op jit(solution)/shard_map/dot_general | solution.py:11
  205.2 1.7 collective-permute-start.13
  207.6 9.4 %all-to-all-start.2 = ((bf16[16,8,112]{2,1,0:T(8,128)(2,1)}), bf16[16,8,112]{2,1,0:T(8,128)(2,1)S(1)}, u32[]{:S(2)}, u32[]{:S(2)}) async-start(bf16[16,8,112]{2,1,0:T(8,128)(2,1)} %bitcast.341), calls=%async_computation.2 | async-start | bytes 65536 | tf_op jit(solution)/shard_map/all_to_all | solution.py:135
  217.0 1.9 fusion.100
  218.9 1.9 fusion.99
  220.8 1.9 fusion.98
  222.6 1.9 fusion.97
  224.5 18.6 %all_gather.15 = bf16[128,2048]{1,0:T(8,128)(2,1)S(1)} all-gather(bf16[8,2048]{1,0:T(8,128)(2,1)S(1)} %pad_maximum_fusion.5), channel_id=1, replica_groups=mesh['leaf'=16,'col'=16] {'col'}, dimensions={0}, use_global_device_ids=true | all-gather | bytes 557056 | tf_op jit(solution)/shard_map/all_gather | solution.py:123
  245.2 4.7 %all-to-all-start.1 = ((bf16[16,112,128]{2,1,0:T(8,128)(2,1)}), bf16[16,112,128]{2,1,0:T(8,128)(2,1)S(1)}, u32[]{:S(2)}, u32[]{:S(2)}) async-start(bf16[16,112,128]{2,1,0:T(8,128)(2,1)} %bitcast.58), calls=%async_computation.1 | async-start | bytes 917504 | tf_op jit(solution)/shard_map/all_to_all | solution.py:132
  250.0 15.7 %all-to-all-done.1 = bf16[16,112,128]{2,1,0:T(8,128)(2,1)S(1)} async-done(((bf16[16,112,128]{2,1,0:T(8,128)(2,1)}), bf16[16,112,128]{2,1,0:T(8,128)(2,1)S(1)}, u32[]{:S(2)}, u32[]{:S(2)}) %all-to-all-start.1) | async-done | bytes 458784 | tf_op jit(solution)/shard_map/all_to_all | solution.py:132
  (116 shorter events, 23.6 us)
Async XLA Ops:
  6.5 32.6 %copy-start = (bf16[1,112,1792]{2,1,0:T(8,128)(2,1)S(1)}, bf16[1,112,1792]{2,1,0:T(8,128)(2,1)}, u32[]{:S(2)}) copy-start(bf16[1,112,1792]{2,1,0:T(8,128)(2,1)} %param.8) | copy-start | bytes 1204228
  6.5 33.9 %copy-start.2 = (bf16[1,4,112,512]{3,2,1,0:T(8,128)(2,1)S(1)}, bf16[1,4,112,512]{3,2,1,0:T(8,128)(2,1)}, u32[]{:S(2)}) copy-start(bf16[1,4,112,512]{3,2,1,0:T(8,128)(2,1)} %param.10) | copy-start | bytes 1376260
  6.5 39.7 %copy-start.12 = (s32[1,2,4,512]{3,2,1,0:T(4,128)S(1)}, s32[1,2,4,512]{3,2,1,0:T(4,128)}, u32[]{:S(2)}) copy-start(s32[1,2,4,512]{3,2,1,0:T(4,128)} %param.13) | copy-start | bytes 49156
  6.5 80.4 %all-gather.6.cloned.1.call-start = ((), (), s32[]{:S(2)}) async-start(), calls=%async_computation.3 | async-start | bytes 6823936 | tf_op jit(solution)/shard_map/all_gather | solution.py:45
  7.3 109.4 %all-gather.8.cloned.1.call-start = ((), (), s32[]{:S(2)}) async-start(), calls=%async_computation.4 | async-start | bytes 5849088 | tf_op jit(solution)/shard_map/all_gather | solution.py:46
  11.9 41.0 %copy-start.13 = (f32[112]{0:T(128)}, f32[112]{0:T(128)S(1)}, u32[]{:S(2)}) copy-start(f32[112]{0:T(128)S(1)} %compare_convert_fusion) | copy-start | bytes 1348
  39.7 0.6 copy-start.10
  42.0 26.5 %all-to-all-start = ((bf16[16,8,2048]{2,1,0:T(8,128)(2,1)}), bf16[16,8,2048]{2,1,0:T(8,128)(2,1)S(1)}, u32[]{:S(2)}, u32[]{:S(2)}) async-start(bf16[16,8,2048]{2,1,0:T(8,128)(2,1)} %pad_maximum_fusion), calls=%async_computation | async-start | bytes 1048576 | tf_op jit(solution)/shard_map/all_to_all | solution.py:58
  76.7 9.3 %collective-permute-start = (f32[4,8,1792]{2,1,0:T(8,128)}, f32[4,8,1792]{2,1,0:T(8,128)}, u32[]{:S(2)}, u32[]{:S(2)}) collective-permute-start(f32[4,8,1792]{2,1,0:T(8,128)} %pad_maximum_fusion.1), channel_id=1, source_target_pairs={{0,16},{32,48},{64,80},{96,112},{128,144},{160,176},{192,208},{224... | collective-permute-start | bytes 688136 | tf_op jit(solution)/shard_map/ppermute | solution.py:76
  79.9 7.1 %copy-start.6 = (bf16[1,1,1792,8]{2,3,1,0:T(8,128)(2,1)}, bf16[1,1,1792,8]{2,3,1,0:T(8,128)(2,1)S(1)}, u32[]{:S(2)}) copy-start(bf16[1,1,1792,8]{2,3,1,0:T(8,128)(2,1)S(1)} %copy.34) | copy-start | bytes 86020
  86.9 0.7 copy-start.4
  93.0 40.3 %slice-start = ((s8[6422528]{0:T(1024)(128)(4,1)}), s8[2228224]{0:T(1024)(128)(4,1)S(1)}, s32[]{:S(2)}) async-start(s8[6422528]{0:T(1024)(128)(4,1)} %bitcast.342), calls=%async_computation.5 | async-start | bytes 4456448
  116.6 6.4 %copy-start.1 = (bf16[1,3,1792,512]{3,2,1,0:T(8,128)(2,1)S(1)}, bf16[1,3,1792,512]{3,2,1,0:T(8,128)(2,1)}, u32[]{:S(2)}) copy-start(bf16[1,3,1792,512]{3,2,1,0:T(8,128)(2,1)} %all-gather.8.cloned.1.call-done) | copy-start | bytes 16515076
  116.6 9.3 %copy-start.5 = (f32[4,8,1792]{2,1,0:T(8,128)S(1)}, f32[4,8,1792]{2,1,0:T(8,128)}, u32[]{:S(2)}) copy-start(f32[4,8,1792]{2,1,0:T(8,128)} %copy-done.4) | copy-start | bytes 688132
  116.6 16.6 %copy-start.7 = (bf16[1,1,1792,8]{2,3,1,0:T(8,128)(2,1)S(1)}, bf16[1,1,1792,8]{2,3,1,0:T(8,128)(2,1)}, u32[]{:S(2)}) copy-start(bf16[1,1,1792,8]{2,3,1,0:T(8,128)(2,1)} %copy-done.6) | copy-start | bytes 86020
  121.1 12.2 %slice-start.1 = ((s8[6422528]{0:T(1024)(128)(4,1)}), s8[4194304]{0:T(1024)(128)(4,1)S(1)}, s32[]{:S(2)}) async-start(s8[6422528]{0:T(1024)(128)(4,1)} %bitcast.342), calls=%async_computation.6 | async-start | bytes 8388608
  126.0 3.8 %collective-permute-start.1 = (f32[3,8,1792]{2,1,0:T(8,128)S(1)}, f32[3,8,1792]{2,1,0:T(8,128)S(1)}, u32[]{:S(2)}, u32[]{:S(2)}) collective-permute-start(f32[3,8,1792]{2,1,0:T(8,128)S(1)} %slice_add_fusion), channel_id=1, source_target_pairs={{16,32},{80,96},{144,160},{208,224},{17,33},{81,97},{145,161},{209... | collective-permute-start | bytes 516104 | tf_op jit(solution)/shard_map/ppermute | solution.py:81
  126.7 6.5 %collective-permute-start.2 = (f32[3,8,1792]{2,1,0:T(8,128)S(1)}, f32[3,8,1792]{2,1,0:T(8,128)S(1)}, u32[]{:S(2)}, u32[]{:S(2)}) collective-permute-start(f32[3,8,1792]{2,1,0:T(8,128)S(1)} %slice_add_fusion), channel_id=1, source_target_pairs={{48,32},{112,96},{176,160},{240,224},{49,33},{113,97},{177,161},{2... | collective-permute-start | bytes 516104 | tf_op jit(solution)/shard_map/ppermute | solution.py:81
  135.1 6.5 %copy-start.8 = (bf16[8,1792]{1,0:T(8,128)(2,1)}, bf16[8,1792]{1,0:T(8,128)(2,1)S(1)}, u32[]{:S(2)}) copy-start(bf16[8,1792]{1,0:T(8,128)(2,1)S(1)} %fusion.74) | copy-start | bytes 86020
  138.2 1.5 collective-permute-start.3
  138.9 0.9 collective-permute-start.4
  141.5 0.9 copy-start.9
  142.5 1.4 collective-permute-start.5
  143.2 0.7 collective-permute-start.6
  152.3 1.3 collective-permute-start.7
  153.0 0.7 collective-permute-start.8
  159.3 1.3 collective-permute-start.10
  159.9 0.7 collective-permute-start.9
  170.2 2.0 collective-permute-start.11
  170.9 21.5 %collective-permute-start.12 = (bf16[3,8,1792]{2,1,0:T(8,128)(2,1)S(1)}, bf16[3,8,1792]{2,1,0:T(8,128)(2,1)S(1)}, u32[]{:S(2)}, u32[]{:S(2)}) collective-permute-start(bf16[3,8,1792]{2,1,0:T(8,128)(2,1)S(1)} %pad_maximum_fusion.3), channel_id=1, source_target_pairs={{32,48},{96,112},{160,176},{224,240},{33,49},{97,113},{161,177},{2... | collective-permute-start | bytes 258056 | tf_op jit(solution)/shard_map/ppermute | solution.py:117
  205.1 38.0 %copy-start.3 = (bf16[1,4,112,512]{3,2,1,0:T(8,128)(2,1)S(1)}, bf16[1,4,112,512]{3,2,1,0:T(8,128)(2,1)}, u32[]{:S(2)}) copy-start(bf16[1,4,112,512]{3,2,1,0:T(8,128)(2,1)} %param.10) | copy-start | bytes 1376260
  205.2 11.8 %collective-permute-start.13 = (bf16[4,8,1792]{2,1,0:T(8,128)(2,1)S(1)}, bf16[4,8,1792]{2,1,0:T(8,128)(2,1)S(1)}, u32[]{:S(2)}, u32[]{:S(2)}) collective-permute-start(bf16[4,8,1792]{2,1,0:T(8,128)(2,1)S(1)} %pad_maximum_fusion.2), channel_id=1, source_target_pairs={{16,0},{48,32},{80,64},{112,96},{144,128},{176,160},{208,192},{240... | collective-permute-start | bytes 344072 | tf_op jit(solution)/shard_map/ppermute | solution.py:112
  207.0 36.7 %copy-start.11 = (bf16[128,112]{0,1:T(8,128)(2,1)S(1)}, bf16[128,112]{0,1:T(8,128)(2,1)}, u32[]{:S(2)}) copy-start(bf16[128,112]{0,1:T(8,128)(2,1)} %copy-done.10) | copy-start | bytes 86020
  207.0 36.7 %copy-start.14 = (f32[112]{0:T(128)S(1)}, f32[112]{0:T(128)}, u32[]{:S(2)}) copy-start(f32[112]{0:T(128)} %copy-done.13) | copy-start | bytes 1348
  207.6 37.6 %all-to-all-start.2 = ((bf16[16,8,112]{2,1,0:T(8,128)(2,1)}), bf16[16,8,112]{2,1,0:T(8,128)(2,1)S(1)}, u32[]{:S(2)}, u32[]{:S(2)}) async-start(bf16[16,8,112]{2,1,0:T(8,128)(2,1)} %bitcast.341), calls=%async_computation.2 | async-start | bytes 65536 | tf_op jit(solution)/shard_map/all_to_all | solution.py:135
  245.2 20.6 %all-to-all-start.1 = ((bf16[16,112,128]{2,1,0:T(8,128)(2,1)}), bf16[16,112,128]{2,1,0:T(8,128)(2,1)S(1)}, u32[]{:S(2)}, u32[]{:S(2)}) async-start(bf16[16,112,128]{2,1,0:T(8,128)(2,1)} %bitcast.58), calls=%async_computation.1 | async-start | bytes 917504 | tf_op jit(solution)/shard_map/all_to_all | solution.py:132
Sparse Core Ops, SparseCore 0:
  9.2 63.2 all-gather.5
  74.3 42.2 all-gather.7
where the time goes:
time: 275 us; the launch traced here: 273 us
  waiting for transfers between devices  83.3 us (30%)
  matrix products  75.3 us (27%)
  blocking collectives  44 us (16%)
  starting transfers between devices  32.5 us (12%)
  between operations  14.1 us (5%)
  other arithmetic  12.3 us (4%)
  local copies, waits for them, and re-layouts  12 us (4%)
    dot_general x43, matrix products, dot(): lax.dot_general(a, b, (((ca,), (cb,)), ((), ())), preferred_element_type=...  75.3 us
    all_gather x1, blocking collectives, shards(): both = lax.all_gather(right_sides[0], 'col', axis=1, tiled=True)  25.3 us
    all_gather x1, waiting for transfers between devices, shards(): lax.all_gather(upper_update[0, :depth - 1], 'col', axis=1, tiled=True)  23.7 us
    ppermute x3, waiting for transfers between devices, shards(): lax.ppermute(above, 'leaf', [(i, i + step) for i in ups])  20.2 us
    all_gather x1, blocking collectives, shards(): tiles = lax.all_gather(tiles, 'col', axis=0, tiled=True)  18.6 us
    all_to_all x1, waiting for transfers between devices, shards(): swapped = lax.all_to_all(terms, 'col', 0, 0, tiled=False)  15.7 us
    all_to_all x1, waiting for transfers between devices, shards(): lax.all_to_all(terms.reshape(col_count, part, depth * tile_len), 'col', 0...  14 us
    all_to_all x1, starting transfers between devices, shards(): lax.all_to_all(x_up.reshape(part, col_count, rows_dev).transpose(1, 0, 2)...  9.38 us
  transfers between devices with their start and end apart: 19, of which 6 were waited for; matrix products, arithmetic and copies ran while one was open for 16% of the time, Pallas kernels for 0%

commit v1 on v0

--- a/solution.py
+++ b/solution.py
@@ -48,7 +48,9 @@
         tile_map[0][:, :, :, None] == lax.broadcasted_iota(jnp.int32, (1, 1, 1, rows), 3)
     ).astype(BF)
     pick_leaf, pick_up = (picks[0], picks[1])
-    both = lax.all_gather(right_sides[0], "col", axis=1, tiled=True)
+    value = right_sides[0]
+    outgoing = jnp.stack([value] * lax.axis_size("col"))
+    both = jnp.concatenate(lax.all_to_all(outgoing, "col", 0, 0), axis=1)
     r_leaf = jnp.where(rows_full < live_rows[0, 0], both[0], jnp.zeros_like(both[0]))
     base_up = lax.dynamic_slice_in_dim(both[1].T, col_id * part, part, 0).astype(F32)
     y_leaf = (dot(leaf_inverse[0], r_leaf, 1, 0) * mask_leaf).astype(BF)

time: 275 us -> 290 us (1.055)
  waiting for transfers between devices: 83.3 us -> 117 us
  blocking collectives: 44 us -> 18.6 us
  starting transfers between devices: 32.5 us -> 42 us
    all_to_all x0 -> x1, waiting for transfers between devices: none -> 30.8 us  [shards(): both = jnp.concatenate(lax.all_to_all(outgoing, 'col', 0, 0), axis=1)]
    all_gather x1 -> x0, blocking collectives: 25.3 us -> none  [shards(): both = lax.all_gather(right_sides[0], 'col', axis=1, tiled=True)]
    all_to_all x0 -> x1, starting transfers between devices: none -> 9.15 us  [shards(): both = jnp.concatenate(lax.all_to_all(outgoing, 'col', 0, 0), axis=1)]
  transfers between devices with their start and end apart: 19 -> 20, of which waited for: 6 -> 7; matrix products, arithmetic and copies ran while one was open for 16% -> 14% of each run, Pallas kernels for 0% -> 0%
where the time goes in v1:
time: 290 us; the launch traced here: 288 us
  waiting for transfers between devices  117 us (40%)
  matrix products  74.9 us (26%)
  starting transfers between devices  42 us (14%)
  blocking collectives  18.6 us (6%)
  between operations  14.1 us (5%)
  other arithmetic  11.1 us (4%)
  local copies, waits for them, and re-layouts  10.2 us (4%)
    dot_general x43, matrix products, dot(): lax.dot_general(a, b, (((ca,), (cb,)), ((), ())), preferred_element_type=...  74.9 us
    all_to_all x1, waiting for transfers between devices, shards(): both = jnp.concatenate(lax.all_to_all(outgoing, 'col', 0, 0), axis=1)  30.8 us
    all_gather x1, waiting for transfers between devices, shards(): lax.all_gather(upper_update[0, :depth - 1], 'col', axis=1, tiled=True)  25.5 us
    ppermute x3, waiting for transfers between devices, shards(): lax.ppermute(above, 'leaf', [(i, i + step) for i in ups])  20.2 us
    all_gather x1, blocking collectives, shards(): tiles = lax.all_gather(tiles, 'col', axis=0, tiled=True)  18.6 us
    all_to_all x1, waiting for transfers between devices, shards(): swapped = lax.all_to_all(terms, 'col', 0, 0, tiled=False)  15.7 us
    all_to_all x1, waiting for transfers between devices, shards(): lax.all_to_all(terms.reshape(col_count, part, depth * tile_len), 'col', 0...  13.3 us
    all_to_all x1, starting transfers between devices, shards(): lax.all_to_all(x_up.reshape(part, col_count, rows_dev).transpose(1, 0, 2)...  9.37 us
  transfers between devices with their start and end apart: 20, of which 7 were waited for; matrix products, arithmetic and copies ran while one was open for 14% of the time, Pallas kernels for 0%

profile of v1, /device:TPU:23, one launch (start us, length us, event | category | flops | bytes accessed | tf_op | source)
XLA Modules:
  0.0 288.1 jit_solution(17616946051565890970)
XLA Ops:
  7.3 1.7 slice.257
  9.1 1.9 stack.49
  11.0 9.2 %all-to-all-start = ((bf16[16,2,112,128]{3,2,1,0:T(8,128)(2,1)}), bf16[16,2,112,128]{3,2,1,0:T(8,128)(2,1)S(1)}, u32[]{:S(2)}, u32[]{:S(2)}) async-start(bf16[16,2,112,128]{3,2,1,0:T(8,128)(2,1)} %stack.49), calls=%async_computation | async-start | bytes 1835008 | tf_op jit(solution)/shard_map/all_to_all | solution.py:53
  20.1 1.3 fusion.218
  22.8 30.8 %all-to-all-done = bf16[16,2,112,128]{3,2,1,0:T(8,128)(2,1)S(1)} async-done(((bf16[16,2,112,128]{3,2,1,0:T(8,128)(2,1)}), bf16[16,2,112,128]{3,2,1,0:T(8,128)(2,1)S(1)}, u32[]{:S(2)}, u32[]{:S(2)}) %all-to-all-start) | async-done | bytes 917536 | tf_op jit(solution)/shard_map/all_to_all | solution.py:53
  56.6 4.5 %all-to-all-start.1 = ((bf16[16,8,2048]{2,1,0:T(8,128)(2,1)}), bf16[16,8,2048]{2,1,0:T(8,128)(2,1)S(1)}, u32[]{:S(2)}, u32[]{:S(2)}) async-start(bf16[16,8,2048]{2,1,0:T(8,128)(2,1)} %pad_maximum_fusion), calls=%async_computation.1 | async-start | bytes 1048576 | tf_op jit(solution)/shard_map/all_to_all | solution.py:60
  61.1 6.7 %iota_compare_fusion = pred[2,4,512,1792]{3,2,1,0:T(32,128)(4,1)} fusion(s32[2,4,512]{2,1,0:T(4,128)S(1)} %bitcast.330), kind=kLoop, calls=%fused_computation | loop fusion | flops 7340032 | bytes 7356416 | tf_op jit(solution)/shard_map/eq | solution.py:48
  68.4 1.6 slice_bitcast_fusion.2
  70.0 13.3 %all-to-all-done.1 = bf16[16,8,2048]{2,1,0:T(8,128)(2,1)S(1)} async-done(((bf16[16,8,2048]{2,1,0:T(8,128)(2,1)}), bf16[16,8,2048]{2,1,0:T(8,128)(2,1)S(1)}, u32[]{:S(2)}, u32[]{:S(2)}) %all-to-all-start.1) | async-done | bytes 524320 | tf_op jit(solution)/shard_map/all_to_all | solution.py:60
  83.5 1.8 fusion.17
  85.3 1.8 fusion.19
  87.1 1.8 fusion.21
  88.9 1.8 fusion.23
  90.8 1.3 collective-permute-start
  92.5 7.4 %collective-permute-done = f32[4,8,1792]{2,1,0:T(8,128)S(1)} collective-permute-done((f32[4,8,1792]{2,1,0:T(8,128)S(1)}, f32[4,8,1792]{2,1,0:T(8,128)S(1)}, u32[]{:S(2)}, u32[]{:S(2)}) %collective-permute-start) | collective-permute-done | bytes 229408 | tf_op jit(solution)/shard_map/ppermute | solution.py:78
  100.6 5.2 %fusion.77 = bf16[8,1792]{1,0:T(8,128)(2,1)} fusion(bf16[1,1792,1792]{2,1,0:T(8,128)(2,1)} %all-gather.5.cloned.1.call-done, f32[4,8,1792]{2,1,0:T(8,128)S(1)} %add_select_fusion, bf16[1792,8]{0,1:T(8,128)(2,1)S(1)} %copy.25, f32[1792]{0:T(1024)S(1)} %fusion.207), kind=kOutput, calls=%fused_computation.60 | convolution fusion | flops 51466240 | bytes 6553600 | tf_op jit(solution)/shard_map/dot_general | solution.py:11
  105.8 25.5 %all-gather.7.cloned.1.call-done = bf16[1,3,1792,512]{3,2,1,0:T(8,128)(2,1)} async-done(((bf16[1,3,112,512]{3,2,1,0:T(8,128)(2,1)}), bf16[1,3,1792,512]{3,2,1,0:T(8,128)(2,1)}) %all-gather.7.cloned.1.call-update) | async-done | bytes 5505040 | tf_op jit(solution)/shard_map/all_gather | solution.py:46
  131.3 2.0 subtract_convert_fusion.5
  133.9 1.9 subtract_convert_fusion.4
  135.8 2.0 fusion.104
  137.8 1.1 subtract_convert_fusion.3
  138.8 1.8 fusion.25
  141.4 3.1 %collective-permute-start.2 = (f32[3,8,1792]{2,1,0:T(8,128)S(1)}, f32[3,8,1792]{2,1,0:T(8,128)S(1)}, u32[]{:S(2)}, u32[]{:S(2)}) collective-permute-start(f32[3,8,1792]{2,1,0:T(8,128)S(1)} %slice_add_fusion), channel_id=1, source_target_pairs={{48,32},{112,96},{176,160},{240,224},{49,33},{113,97},{177,161},{2... | collective-permute-start | bytes 516104 | tf_op jit(solution)/shard_map/ppermute | solution.py:83
  144.5 3.4 %collective-permute-done.2 = f32[3,8,1792]{2,1,0:T(8,128)S(1)} collective-permute-done((f32[3,8,1792]{2,1,0:T(8,128)S(1)}, f32[3,8,1792]{2,1,0:T(8,128)S(1)}, u32[]{:S(2)}, u32[]{:S(2)}) %collective-permute-start.2) | collective-permute-done | bytes 172064 | tf_op jit(solution)/shard_map/ppermute | solution.py:83
  148.0 1.8 fusion.74
  151.0 1.8 fusion.103
  154.3 1.8 fusion.71
  158.6 4.6 %fusion.86 = f32[8,1792]{1,0:T(8,128)S(1)} fusion(bf16[1,1792,1792]{2,1,0:T(8,128)(2,1)} %all-gather.5.cloned.1.call-done, bf16[1792,8]{0,1:T(8,128)(2,1)} %copy-done.6, f32[1,8,1792]{2,1,0:T(8,128)S(1)} %collective-permute-done.5, f32[1,8,1792]{2,1,0:T(8,128)S(1)} %collective-permute-done.6, bf16[8,1792]{1,0:T(8,128)(2,1)} %copy-done.9, ...), kind=kOutput, calls=%fused_computation.65 | convolution fusion | flops 51552256 | bytes 6716420 | tf_op jit(solution)/shard_map/dot_general | solution.py:11
  163.2 3.8 %fusion.65 = bf16[8,1792]{1,0:T(8,128)(2,1)S(1)} fusion(bf16[1,1792,1792]{2,1,0:T(8,128)(2,1)} %all-gather.5.cloned.1.call-done, f32[8,1792]{1,0:T(8,128)S(1)} %fusion.86, f32[1792]{0:T(1024)S(1)} %fusion.207), kind=kOutput, calls=%fused_computation.56 | convolution fusion | flops 51437568 | bytes 6515712 | tf_op jit(solution)/shard_map/dot_general | solution.py:11
  169.0 4.9 %fusion.62 = bf16[8,1792]{1,0:T(8,128)(2,1)S(1)} fusion(bf16[1,1792,1792]{2,1,0:T(8,128)(2,1)} %all-gather.5.cloned.1.call-done, f32[8,1792]{1,0:T(8,128)S(1)} %fusion.86, bf16[8,512]{1,0:T(8,128)(2,1)S(1)} %convolution_convert_fusion.9, bf16[1,3,1792,512]{3,2,1,0:T(8,128)(2,1)} %all-gather.7.cloned.1.call-done, f32[1792]{0:T(1024)S(1)} %fusion.207), kind=kOutput, calls=%fused_computation.55 | convolution fusion | flops 66131968 | bytes 8368128 | tf_op jit(solution)/shard_map/dot_general | solution.py:11
  175.4 2.7 fusion.101
  178.0 3.1 %fusion.81 = bf16[8,1792]{1,0:T(8,128)(2,1)S(1)} fusion(f32[8,1792]{1,0:T(8,128)S(1)} %fusion.86, f32[8,1792]{1,0:T(8,128)S(1)} %fusion.101, bf16[1,3,1792,512]{3,2,1,0:T(8,128)(2,1)} %all-gather.7.cloned.1.call-done, pred[2,4,512,1792]{3,2,1,0:T(32,128)(4,1)} %iota_compare_fusion, bf16[2,8,1792]{2,1,0:T(8,128)(2,1)S(1)} %add.145, f32[1792]{0:T(1024)S(1)} %fusion.207), kind=kOutput, calls=%fused_computation.62 | convolution fusion | flops 29421568 | bytes 2932736 | tf_op jit(solution)/shard_map/dot_general | solution.py:11
  181.1 3.8 %fusion.59 = bf16[8,1792]{1,0:T(8,128)(2,1)S(1)} fusion(bf16[8,1792]{1,0:T(8,128)(2,1)S(1)} %fusion.81, bf16[1,1792,1792]{2,1,0:T(8,128)(2,1)} %all-gather.5.cloned.1.call-done, f32[1792]{0:T(1024)S(1)} %fusion.207), kind=kOutput, calls=%fused_computation.54 | convolution fusion | flops 51408896 | bytes 6487040 | tf_op jit(solution)/shard_map/dot_general | solution.py:11
  185.6 1.3 collective-permute-start.12
  186.9 20.2 %collective-permute-done.12 = bf16[3,8,1792]{2,1,0:T(8,128)(2,1)S(1)} collective-permute-done((bf16[3,8,1792]{2,1,0:T(8,128)(2,1)S(1)}, bf16[3,8,1792]{2,1,0:T(8,128)(2,1)S(1)}, u32[]{:S(2)}, u32[]{:S(2)}) %collective-permute-start.12) | collective-permute-done | bytes 86048 | tf_op jit(solution)/shard_map/ppermute | solution.py:119
  207.2 2.7 fusion.102
  209.8 3.1 %convolution_add_fusion.1 = f32[8,1792]{1,0:T(8,128)S(1)} fusion(f32[8,1792]{1,0:T(8,128)S(1)} %fusion.102, bf16[1,3,1792,512]{3,2,1,0:T(8,128)(2,1)} %all-gather.7.cloned.1.call-done, pred[2,4,512,1792]{3,2,1,0:T(32,128)(4,1)} %iota_compare_fusion, bf16[3,8,1792]{2,1,0:T(8,128)(2,1)S(1)} %add.147), kind=kOutput, calls=%fused_computation.39 | convolution fusion | flops 29378560 | bytes 2895872 | tf_op jit(solution)/shard_map/dot_general | solution.py:11
  213.0 3.1 %fusion.82 = bf16[8,1792]{1,0:T(8,128)(2,1)S(1)} fusion(f32[8,1792]{1,0:T(8,128)S(1)} %fusion.86, f32[8,1792]{1,0:T(8,128)S(1)} %convolution_add_fusion.1, bf16[1,3,1792,512]{3,2,1,0:T(8,128)(2,1)} %all-gather.7.cloned.1.call-done, pred[2,4,512,1792]{3,2,1,0:T(32,128)(4,1)} %iota_compare_fusion, bf16[3,8,1792]{2,1,0:T(8,128)(2,1)S(1)} %add.147, ...), kind=kOutput, calls=%fused_computation.63 | convolution fusion | flops 29421568 | bytes 2932736 | tf_op jit(solution)/shard_map/dot_general | solution.py:11
  216.1 3.8 %select_select_fusion = (bf16[8,1792]{1,0:T(8,128)(2,1)S(1)}, bf16[8,1792]{1,0:T(8,128)(2,1)S(1)}) fusion(bf16[8,1792]{1,0:T(8,128)(2,1)S(1)} %fusion.59, bf16[8,1792]{1,0:T(8,128)(2,1)S(1)} %fusion.62, bf16[8,1792]{1,0:T(8,128)(2,1)S(1)} %fusion.65, pred[]{:T(512)S(6)} %gt.2, pred[]{:T(512)S(6)} %eq.63, pred[]{:T(512)S(6)} %eq.62, pred[]{:T(512)S(6)} %eq.61, ...), kind=kOutput, calls=%fused_computation.194 | convolution fusion | flops 51480576 | bytes 6601733 | tf_op jit(solution)/shard_map/dot_general | solution.py:11
  219.9 1.7 collective-permute-start.13
  222.3 9.4 %all-to-all-start.3 = ((bf16[16,8,112]{2,1,0:T(8,128)(2,1)}), bf16[16,8,112]{2,1,0:T(8,128)(2,1)S(1)}, u32[]{:S(2)}, u32[]{:S(2)}) async-start(bf16[16,8,112]{2,1,0:T(8,128)(2,1)} %bitcast.315), calls=%async_computation.3 | async-start | bytes 65536 | tf_op jit(solution)/shard_map/all_to_all | solution.py:137
  231.7 1.9 fusion.100
  233.6 1.9 fusion.99
  235.5 1.9 fusion.98
  237.3 1.9 fusion.97
  239.2 18.6 %all_gather.11 = bf16[128,2048]{1,0:T(8,128)(2,1)S(1)} all-gather(bf16[8,2048]{1,0:T(8,128)(2,1)S(1)} %pad_maximum_fusion.5), channel_id=1, replica_groups=mesh['leaf'=16,'col'=16] {'col'}, dimensions={0}, use_global_device_ids=true | all-gather | bytes 557056 | tf_op jit(solution)/shard_map/all_gather | solution.py:125
  259.9 4.7 %all-to-all-start.2 = ((bf16[16,112,128]{2,1,0:T(8,128)(2,1)}), bf16[16,112,128]{2,1,0:T(8,128)(2,1)S(1)}, u32[]{:S(2)}, u32[]{:S(2)}) async-start(bf16[16,112,128]{2,1,0:T(8,128)(2,1)} %bitcast.58), calls=%async_computation.2 | async-start | bytes 917504 | tf_op jit(solution)/shard_map/all_to_all | solution.py:134
  264.8 15.7 %all-to-all-done.2 = bf16[16,112,128]{2,1,0:T(8,128)(2,1)S(1)} async-done(((bf16[16,112,128]{2,1,0:T(8,128)(2,1)}), bf16[16,112,128]{2,1,0:T(8,128)(2,1)S(1)}, u32[]{:S(2)}, u32[]{:S(2)}) %all-to-all-start.2) | async-done | bytes 458784 | tf_op jit(solution)/shard_map/all_to_all | solution.py:134
  (118 shorter events, 21.0 us)
Async XLA Ops:
  6.5 47.5 %copy-start = (bf16[1,112,1792]{2,1,0:T(8,128)(2,1)S(1)}, bf16[1,112,1792]{2,1,0:T(8,128)(2,1)}, u32[]{:S(2)}) copy-start(bf16[1,112,1792]{2,1,0:T(8,128)(2,1)} %param.8) | copy-start | bytes 1204228
  6.5 48.5 %copy-start.2 = (bf16[1,4,112,512]{3,2,1,0:T(8,128)(2,1)S(1)}, bf16[1,4,112,512]{3,2,1,0:T(8,128)(2,1)}, u32[]{:S(2)}) copy-start(bf16[1,4,112,512]{3,2,1,0:T(8,128)(2,1)} %param.10) | copy-start | bytes 1376260
  6.5 54.5 %copy-start.12 = (s32[1,2,4,512]{3,2,1,0:T(4,128)S(1)}, s32[1,2,4,512]{3,2,1,0:T(4,128)}, u32[]{:S(2)}) copy-start(s32[1,2,4,512]{3,2,1,0:T(4,128)} %param.13) | copy-start | bytes 49156
  6.5 93.4 %all-gather.5.cloned.1.call-start = ((), (), s32[]{:S(2)}) async-start(), calls=%async_computation.4 | async-start | bytes 6823936 | tf_op jit(solution)/shard_map/all_gather | solution.py:45
  7.3 124.1 %all-gather.7.cloned.1.call-start = ((), (), s32[]{:S(2)}) async-start(), calls=%async_computation.5 | async-start | bytes 5849088 | tf_op jit(solution)/shard_map/all_gather | solution.py:46
  11.0 42.7 %all-to-all-start = ((bf16[16,2,112,128]{3,2,1,0:T(8,128)(2,1)}), bf16[16,2,112,128]{3,2,1,0:T(8,128)(2,1)S(1)}, u32[]{:S(2)}, u32[]{:S(2)}) async-start(bf16[16,2,112,128]{3,2,1,0:T(8,128)(2,1)} %stack.49), calls=%async_computation | async-start | bytes 1835008 | tf_op jit(solution)/shard_map/all_to_all | solution.py:53
  22.1 45.7 %copy-start.13 = (f32[112]{0:T(128)}, f32[112]{0:T(128)S(1)}, u32[]{:S(2)}) copy-start(f32[112]{0:T(128)S(1)} %compare_convert_fusion) | copy-start | bytes 1348
  54.3 0.6 copy-start.10
  56.6 26.8 %all-to-all-start.1 = ((bf16[16,8,2048]{2,1,0:T(8,128)(2,1)}), bf16[16,8,2048]{2,1,0:T(8,128)(2,1)S(1)}, u32[]{:S(2)}, u32[]{:S(2)}) async-start(bf16[16,8,2048]{2,1,0:T(8,128)(2,1)} %pad_maximum_fusion), calls=%async_computation.1 | async-start | bytes 1048576 | tf_op jit(solution)/shard_map/all_to_all | solution.py:60
  90.8 9.1 %collective-permute-start = (f32[4,8,1792]{2,1,0:T(8,128)S(1)}, f32[4,8,1792]{2,1,0:T(8,128)S(1)}, u32[]{:S(2)}, u32[]{:S(2)}) collective-permute-start(f32[4,8,1792]{2,1,0:T(8,128)S(1)} %pad_maximum_fusion.1), channel_id=1, source_target_pairs={{0,16},{32,48},{64,80},{96,112},{128,144},{160,176},{192,208},{224... | collective-permute-start | bytes 688136 | tf_op jit(solution)/shard_map/ppermute | solution.py:78
  92.5 7.5 %copy-start.6 = (bf16[1792,8]{0,1:T(8,128)(2,1)}, bf16[1792,8]{0,1:T(8,128)(2,1)S(1)}, u32[]{:S(2)}) copy-start(bf16[1792,8]{0,1:T(8,128)(2,1)S(1)} %copy.25) | copy-start | bytes 86020
  99.9 0.7 copy-start.4
  105.8 42.2 %slice-start = ((s8[6422528]{0:T(1024)(128)(4,1)}), s8[2228224]{0:T(1024)(128)(4,1)S(1)}, s32[]{:S(2)}) async-start(s8[6422528]{0:T(1024)(128)(4,1)} %bitcast.316), calls=%async_computation.6 | async-start | bytes 4456448
  131.3 6.4 %copy-start.1 = (bf16[1,3,1792,512]{3,2,1,0:T(8,128)(2,1)S(1)}, bf16[1,3,1792,512]{3,2,1,0:T(8,128)(2,1)}, u32[]{:S(2)}) copy-start(bf16[1,3,1792,512]{3,2,1,0:T(8,128)(2,1)} %all-gather.7.cloned.1.call-done) | copy-start | bytes 16515076
  131.3 9.3 %copy-start.5 = (f32[4,8,1792]{2,1,0:T(8,128)S(1)}, f32[4,8,1792]{2,1,0:T(8,128)}, u32[]{:S(2)}) copy-start(f32[4,8,1792]{2,1,0:T(8,128)} %copy-done.4) | copy-start | bytes 688132
  131.3 16.6 %copy-start.7 = (bf16[1792,8]{0,1:T(8,128)(2,1)S(1)}, bf16[1792,8]{0,1:T(8,128)(2,1)}, u32[]{:S(2)}) copy-start(bf16[1792,8]{0,1:T(8,128)(2,1)} %copy-done.6) | copy-start | bytes 86020
  135.8 12.2 %slice-start.1 = ((s8[6422528]{0:T(1024)(128)(4,1)}), s8[4194304]{0:T(1024)(128)(4,1)S(1)}, s32[]{:S(2)}) async-start(s8[6422528]{0:T(1024)(128)(4,1)} %bitcast.316), calls=%async_computation.7 | async-start | bytes 8388608
  140.7 3.8 %collective-permute-start.1 = (f32[3,8,1792]{2,1,0:T(8,128)S(1)}, f32[3,8,1792]{2,1,0:T(8,128)S(1)}, u32[]{:S(2)}, u32[]{:S(2)}) collective-permute-start(f32[3,8,1792]{2,1,0:T(8,128)S(1)} %slice_add_fusion), channel_id=1, source_target_pairs={{16,32},{80,96},{144,160},{208,224},{17,33},{81,97},{145,161},{209... | collective-permute-start | bytes 516104 | tf_op jit(solution)/shard_map/ppermute | solution.py:83
  141.4 6.5 %collective-permute-start.2 = (f32[3,8,1792]{2,1,0:T(8,128)S(1)}, f32[3,8,1792]{2,1,0:T(8,128)S(1)}, u32[]{:S(2)}, u32[]{:S(2)}) collective-permute-start(f32[3,8,1792]{2,1,0:T(8,128)S(1)} %slice_add_fusion), channel_id=1, source_target_pairs={{48,32},{112,96},{176,160},{240,224},{49,33},{113,97},{177,161},{2... | collective-permute-start | bytes 516104 | tf_op jit(solution)/shard_map/ppermute | solution.py:83
  149.8 6.3 %copy-start.8 = (bf16[8,1792]{1,0:T(8,128)(2,1)}, bf16[8,1792]{1,0:T(8,128)(2,1)S(1)}, u32[]{:S(2)}) copy-start(bf16[8,1792]{1,0:T(8,128)(2,1)S(1)} %fusion.74) | copy-start | bytes 86020
  152.9 1.3 collective-permute-start.3
  153.6 0.7 collective-permute-start.4
  156.1 0.9 copy-start.9
  157.0 1.6 collective-permute-start.5
  157.7 0.9 collective-permute-start.6
  167.0 1.3 collective-permute-start.7
  167.7 0.7 collective-permute-start.8
  174.0 1.3 collective-permute-start.10
  174.6 0.7 collective-permute-start.9
  184.9 2.0 collective-permute-start.11
  185.6 21.5 %collective-permute-start.12 = (bf16[3,8,1792]{2,1,0:T(8,128)(2,1)S(1)}, bf16[3,8,1792]{2,1,0:T(8,128)(2,1)S(1)}, u32[]{:S(2)}, u32[]{:S(2)}) collective-permute-start(bf16[3,8,1792]{2,1,0:T(8,128)(2,1)S(1)} %pad_maximum_fusion.3), channel_id=1, source_target_pairs={{32,48},{96,112},{160,176},{224,240},{33,49},{97,113},{161,177},{2... | collective-permute-start | bytes 258056 | tf_op jit(solution)/shard_map/ppermute | solution.py:119
  219.9 38.0 %copy-start.3 = (bf16[1,4,112,512]{3,2,1,0:T(8,128)(2,1)S(1)}, bf16[1,4,112,512]{3,2,1,0:T(8,128)(2,1)}, u32[]{:S(2)}) copy-start(bf16[1,4,112,512]{3,2,1,0:T(8,128)(2,1)} %param.10) | copy-start | bytes 1376260
  219.9 11.8 %collective-permute-start.13 = (bf16[4,8,1792]{2,1,0:T(8,128)(2,1)S(1)}, bf16[4,8,1792]{2,1,0:T(8,128)(2,1)S(1)}, u32[]{:S(2)}, u32[]{:S(2)}) collective-permute-start(bf16[4,8,1792]{2,1,0:T(8,128)(2,1)S(1)} %pad_maximum_fusion.2), channel_id=1, source_target_pairs={{16,0},{48,32},{80,64},{112,96},{144,128},{176,160},{208,192},{240... | collective-permute-start | bytes 344072 | tf_op jit(solution)/shard_map/ppermute | solution.py:114
  221.7 36.7 %copy-start.11 = (bf16[128,112]{0,1:T(8,128)(2,1)S(1)}, bf16[128,112]{0,1:T(8,128)(2,1)}, u32[]{:S(2)}) copy-start(bf16[128,112]{0,1:T(8,128)(2,1)} %copy-done.10) | copy-start | bytes 86020
  221.7 36.7 %copy-start.14 = (f32[112]{0:T(128)S(1)}, f32[112]{0:T(128)}, u32[]{:S(2)}) copy-start(f32[112]{0:T(128)} %copy-done.13) | copy-start | bytes 1348
  222.3 37.6 %all-to-all-start.3 = ((bf16[16,8,112]{2,1,0:T(8,128)(2,1)}), bf16[16,8,112]{2,1,0:T(8,128)(2,1)S(1)}, u32[]{:S(2)}, u32[]{:S(2)}) async-start(bf16[16,8,112]{2,1,0:T(8,128)(2,1)} %bitcast.315), calls=%async_computation.3 | async-start | bytes 65536 | tf_op jit(solution)/shard_map/all_to_all | solution.py:137
  259.9 20.6 %all-to-all-start.2 = ((bf16[16,112,128]{2,1,0:T(8,128)(2,1)}), bf16[16,112,128]{2,1,0:T(8,128)(2,1)S(1)}, u32[]{:S(2)}, u32[]{:S(2)}) async-start(bf16[16,112,128]{2,1,0:T(8,128)(2,1)} %bitcast.58), calls=%async_computation.2 | async-start | bytes 917504 | tf_op jit(solution)/shard_map/all_to_all | solution.py:134
Sparse Core Ops, SparseCore 0:
  9.2 77.6 all-gather.4
  88.7 42.5 all-gather.6
